TPU v7x, 32 devices: a whole 2x2x4 slice. The times are simulated.
32 devices in a mesh: dp: 4 (over z), fsdp: 8 (over y, x, core).
Axes of the slice: x: 2, y: 2, z: 4, core: 2. Of those that a mesh axis runs over, the one named last changes fastest.
Arguments:
- dec_in: bfloat16 [64, 176, 768], P(('dp', 'fsdp')), may hold values from -6 to 6
- enc_out: bfloat16 [64, 512, 768], P(('dp', 'fsdp')), may hold values from -6 to 6
- seg_dec: int32 [64, 176], P(('dp', 'fsdp')), may hold values from 0 to 4, as said below
- seg_enc: int32 [64, 512], P(('dp', 'fsdp')), may hold values from 0 to 4, as said below
- out_grad: bfloat16 [64, 176, 768], P(('dp', 'fsdp')), may hold values from -6 to 6
- gain_self: bfloat16 [768], P('fsdp'), may hold values from 0.099609375 to 1.8984375
- wq_self: bfloat16 [768, 768], P('fsdp'), may hold values from -0.21875 to 0.21875
- wk_self: bfloat16 [768, 768], P('fsdp'), may hold values from -0.21875 to 0.21875
- wv_self: bfloat16 [768, 768], P('fsdp'), may hold values from -0.21875 to 0.21875
- wo_self: bfloat16 [768, 768], P('fsdp'), may hold values from -1.5 to 1.5
- gain_cross: bfloat16 [768], P('fsdp'), may hold values from 0.099609375 to 1.8984375
- wq_cross: bfloat16 [768, 768], P('fsdp'), may hold values from -0.21875 to 0.21875
- wk_cross: bfloat16 [768, 768], P('fsdp'), may hold values from -0.21875 to 0.21875
- wv_cross: bfloat16 [768, 768], P('fsdp'), may hold values from -0.21875 to 0.21875
- wo_cross: bfloat16 [768, 768], P('fsdp'), may hold values from -2.5 to 2.5
- gain_ffn: bfloat16 [768], P('fsdp'), may hold values from 0.099609375 to 1.8984375
- w_gate: bfloat16 [768, 2048], P('fsdp'), may hold values from -0.21875 to 0.21875
- w_up: bfloat16 [768, 2048], P('fsdp'), may hold values from -0.21875 to 0.21875
- w_down: bfloat16 [2048, 768], P('fsdp'), may hold values from -0.125 to 0.125
Outputs:
- dec_out: bfloat16 [64, 176, 768], P(('dp', 'fsdp'))
- grad_dec: float32 [64, 176, 768], P(('dp', 'fsdp'))
- grad_enc: float32 [64, 512, 768], P(('dp', 'fsdp'))
- grad_gain_self: float32 [768], P('fsdp')
- grad_wq_self: float32 [768, 768], P('fsdp')
- grad_wk_self: float32 [768, 768], P('fsdp')
- grad_wv_self: float32 [768, 768], P('fsdp')
- grad_wo_self: float32 [768, 768], P('fsdp')
- grad_gain_cross: float32 [768], P('fsdp')
- grad_wq_cross: float32 [768, 768], P('fsdp')
- grad_wk_cross: float32 [768, 768], P('fsdp')
- grad_wv_cross: float32 [768, 768], P('fsdp')
- grad_wo_cross: float32 [768, 768], P('fsdp')
- grad_gain_ffn: float32 [768], P('fsdp')
- grad_w_gate: float32 [768, 2048], P('fsdp')
- grad_w_up: float32 [768, 2048], P('fsdp')
- grad_w_down: float32 [2048, 768], P('fsdp')
Inputs may be any that keep to these rules, and one draw needn't show every extreme that they name: `seg_dec`: each row holds segments 1, 2, 3, 4 in this order, each present in both its decoder and its encoder tokens, then 1 to 176 // 16 (decoder) or 512 // 16 (encoder) padding tokens of segment 0 at its end. `seg_enc`: as for seg_dec, with the same segments present.
All inputs are finite; a program needn't handle non-finite values.
Results may differ from a plain program's by a relative error of at most 0.023.
Values may be sent and summed in bfloat16 or wider, within the bound.
A program may use at most 192 MiB of HBM per device.

v0:
```python
import jax
import jax.numpy as jnp
from jax import lax
from jax.sharding import PartitionSpec as P

HD = 64
EPSILON = 1e-06
MASKED = -1000000000.0


def rms_forward(values_in, gain_vec):
    return (
        values_in
        * lax.rsqrt(jnp.mean(values_in * values_in, axis=-1, keepdims=True) + EPSILON)
        * gain_vec
    )


def rms_backward(values_in, gain_low, grad_out):
    _, pullback = jax.vjp(rms_forward, values_in, gain_low.astype(jnp.float32))
    return pullback(grad_out)


def project(acts, weight):
    return jnp.einsum("rld,dn->rln", acts, weight, preferred_element_type=jnp.float32)


def weight_grad(acts, grad_out):
    return jnp.einsum("rld,rln->dn", acts, grad_out, preferred_element_type=jnp.float32)


def input_grad(grad_out, weight):
    return jnp.einsum("rln,dn->rld", grad_out, weight, preferred_element_type=jnp.float32)


def split_heads(tensor):
    return tensor.reshape(tensor.shape[0], tensor.shape[1], -1, HD)


def merge_heads(tensor):
    return tensor.reshape(tensor.shape[0], tensor.shape[1], -1)


def masked_scores(queries, keys_all, allowed):
    raw_scores = jnp.einsum(
        "rqhd,rkhd->rhqk",
        split_heads(queries),
        split_heads(keys_all),
        preferred_element_type=jnp.float32,
    ) * HD ** (-0.5)
    return jnp.where(allowed[:, None], raw_scores, MASKED)


def attend_forward(queries, keys_all, values, allowed):
    scores = masked_scores(queries, keys_all, allowed)
    maxima = jnp.max(scores, axis=-1, keepdims=True)
    log_total = maxima + jnp.log(jnp.sum(jnp.exp(scores - maxima), axis=-1, keepdims=True))
    weights_low = jnp.exp(scores - log_total).astype(jnp.bfloat16)
    mixture = jnp.einsum(
        "rhqk,rkhd->rqhd", weights_low, split_heads(values), preferred_element_type=jnp.float32
    )
    return (merge_heads(mixture).astype(jnp.bfloat16), log_total)


def attend_backward(queries, keys_all, values, allowed, log_total, grad_mix):
    scores = masked_scores(queries, keys_all, allowed)
    weights_full = jnp.exp(scores - log_total)
    grad_heads = split_heads(grad_mix)
    grad_values = jnp.einsum(
        "rhqk,rqhd->rkhd",
        weights_full.astype(jnp.bfloat16),
        grad_heads,
        preferred_element_type=jnp.float32,
    )
    grad_weights = jnp.einsum(
        "rqhd,rkhd->rhqk", grad_heads, split_heads(values), preferred_element_type=jnp.float32
    )
    grad_scores = (
        weights_full * (grad_weights - jnp.sum(weights_full * grad_weights, axis=-1, keepdims=True))
    ).astype(jnp.bfloat16)
    grad_queries = jnp.einsum(
        "rhqk,rkhd->rqhd", grad_scores, split_heads(keys_all), preferred_element_type=jnp.float32
    ) * HD ** (-0.5)
    grad_keys = jnp.einsum(
        "rhqk,rqhd->rkhd", grad_scores, split_heads(queries), preferred_element_type=jnp.float32
    ) * HD ** (-0.5)
    return (
        merge_heads(grad_queries).astype(jnp.bfloat16),
        merge_heads(grad_keys).astype(jnp.bfloat16),
        merge_heads(grad_values).astype(jnp.bfloat16),
    )


def gather_group(shards):
    joined = jnp.concatenate(shards, axis=0)
    whole = lax.all_gather(joined, "fsdp", axis=0, tiled=False)
    parts = []
    start = 0
    for shard in shards:
        part = whole[:, start : start + shard.shape[0]]
        parts.append(part.reshape((-1,) + shard.shape[1:]))
        start += shard.shape[0]
    return parts


def reduce_group(gradients, shards):
    count = lax.axis_size("fsdp")
    joined = jnp.concatenate(
        [
            gradient.astype(jnp.bfloat16).reshape((count, -1) + gradient.shape[1:])
            for gradient in gradients
        ],
        axis=1,
    )
    owned = lax.psum_scatter(joined, "fsdp", scatter_dimension=0, tiled=False)
    quarter = lax.psum_scatter(owned, "dp", scatter_dimension=0, tiled=True)
    summed = lax.all_gather(quarter, "dp", axis=0, tiled=True)
    parts = []
    start = 0
    for shard in shards:
        part = summed[start : start + shard.shape[0]]
        parts.append(part.astype(jnp.float32))
        start += shard.shape[0]
    return parts


def micro_step(
    dec_rows, enc_rows, seg_rows_dec, seg_rows_enc, grad_rows, get_self, get_cross, get_ffn
):
    position = jnp.arange(seg_rows_dec.shape[1])
    causal = position[:, None] >= position[None, :]
    self_ok = (seg_rows_dec[:, :, None] == seg_rows_dec[:, None, :]) & causal[None]
    cross_ok = seg_rows_dec[:, :, None] == seg_rows_enc[:, None, :]
    gain_a, wq_a, wk_a, wv_a, wo_a = get_self()
    dec_float = dec_rows.astype(jnp.float32)
    normed_a = rms_forward(dec_float, gain_a.astype(jnp.float32)).astype(jnp.bfloat16)
    query_a = project(normed_a, wq_a).astype(jnp.bfloat16)
    keys_a = project(normed_a, wk_a).astype(jnp.bfloat16)
    values_a = project(normed_a, wv_a).astype(jnp.bfloat16)
    mix_a, total_a = attend_forward(query_a, keys_a, values_a, self_ok)
    after_self = dec_float + project(mix_a, wo_a)
    gain_c, wq_c, wk_c, wv_c, wo_c = get_cross()
    normed_c = rms_forward(after_self, gain_c.astype(jnp.float32)).astype(jnp.bfloat16)
    query_c = project(normed_c, wq_c).astype(jnp.bfloat16)
    keys_c = project(enc_rows, wk_c).astype(jnp.bfloat16)
    values_c = project(enc_rows, wv_c).astype(jnp.bfloat16)
    mix_c, total_c = attend_forward(query_c, keys_c, values_c, cross_ok)
    after_cross = after_self + project(mix_c, wo_c)
    gain_f, gate_w, up_w, down_w = get_ffn()
    normed_f = rms_forward(after_cross, gain_f.astype(jnp.float32)).astype(jnp.bfloat16)
    gate_pre = project(normed_f, gate_w)
    up_pre = project(normed_f, up_w)
    hidden_low = (jax.nn.gelu(gate_pre, approximate=True) * up_pre).astype(jnp.bfloat16)
    dec_result = (after_cross + project(hidden_low, down_w)).astype(jnp.bfloat16)
    gain_f, gate_w, up_w, down_w = get_ffn()
    grad_res = grad_rows.astype(jnp.float32)
    grad_branch = grad_res.astype(jnp.bfloat16)
    grad_down = weight_grad(hidden_low, grad_branch)
    grad_hidden = input_grad(grad_branch, down_w)
    _, gelu_pull = jax.vjp(
        lambda gate_in, up_in: jax.nn.gelu(gate_in, approximate=True) * up_in, gate_pre, up_pre
    )
    grad_gate_pre, grad_up_pre = gelu_pull(grad_hidden)
    grad_gate_low = grad_gate_pre.astype(jnp.bfloat16)
    grad_up_low = grad_up_pre.astype(jnp.bfloat16)
    grad_gate = weight_grad(normed_f, grad_gate_low)
    grad_up = weight_grad(normed_f, grad_up_low)
    grad_normed = input_grad(grad_gate_low, gate_w) + input_grad(grad_up_low, up_w)
    grad_input, grad_gain_f = rms_backward(after_cross, gain_f, grad_normed)
    grad_res = grad_res + grad_input
    gain_c, wq_c, wk_c, wv_c, wo_c = get_cross()
    grad_branch = grad_res.astype(jnp.bfloat16)
    grad_wo_c = weight_grad(mix_c, grad_branch)
    grad_mix = input_grad(grad_branch, wo_c).astype(jnp.bfloat16)
    grad_query, grad_keys, grad_values = attend_backward(
        query_c, keys_c, values_c, cross_ok, total_c, grad_mix
    )
    grad_wq_c = weight_grad(normed_c, grad_query)
    grad_wk_c = weight_grad(enc_rows, grad_keys)
    grad_wv_c = weight_grad(enc_rows, grad_values)
    grad_enc_rows = input_grad(grad_keys, wk_c) + input_grad(grad_values, wv_c)
    grad_normed = input_grad(grad_query, wq_c)
    grad_input, grad_gain_c = rms_backward(after_self, gain_c, grad_normed)
    grad_res = grad_res + grad_input
    gain_a, wq_a, wk_a, wv_a, wo_a = get_self()
    grad_branch = grad_res.astype(jnp.bfloat16)
    grad_wo_a = weight_grad(mix_a, grad_branch)
    grad_mix = input_grad(grad_branch, wo_a).astype(jnp.bfloat16)
    grad_query, grad_keys, grad_values = attend_backward(
        query_a, keys_a, values_a, self_ok, total_a, grad_mix
    )
    grad_wq_a = weight_grad(normed_a, grad_query)
    grad_wk_a = weight_grad(normed_a, grad_keys)
    grad_wv_a = weight_grad(normed_a, grad_values)
    grad_normed = (
        input_grad(grad_query, wq_a) + input_grad(grad_keys, wk_a) + input_grad(grad_values, wv_a)
    )
    grad_input, grad_gain_a = rms_backward(dec_float, gain_a, grad_normed)
    grad_dec_rows = grad_res + grad_input
    full_grads = (
        grad_gain_a,
        grad_wq_a,
        grad_wk_a,
        grad_wv_a,
        grad_wo_a,
        grad_gain_c,
        grad_wq_c,
        grad_wk_c,
        grad_wv_c,
        grad_wo_c,
        grad_gain_f,
        grad_gate,
        grad_up,
        grad_down,
    )
    return (dec_result, grad_dec_rows, grad_enc_rows, full_grads)


def body(
    dec_in,
    enc_out,
    seg_dec,
    seg_enc,
    out_grad,
    gain_self,
    wq_self,
    wk_self,
    wv_self,
    wo_self,
    gain_cross,
    wq_cross,
    wk_cross,
    wv_cross,
    wo_cross,
    gain_ffn,
    w_gate,
    w_up,
    w_down,
):
    narrow = (wq_self, wk_self, wv_self, wo_self, wq_cross, wk_cross, wv_cross, wo_cross, w_down)
    gain_a, gain_c, gain_f = gather_group((gain_self, gain_cross, gain_ffn))
    full = gather_group(narrow)
    gate_full, up_full = gather_group((w_gate, w_up))
    get_self = lambda: (gain_a, *full[0:4])
    get_cross = lambda: (gain_c, *full[4:8])
    get_ffn = lambda: (gain_f, gate_full, up_full, full[8])
    result_rows, grad_rows_dec, grad_rows_enc, grads = micro_step(
        dec_in, enc_out, seg_dec, seg_enc, out_grad, get_self, get_cross, get_ffn
    )
    gains = reduce_group((grads[0], grads[5], grads[10]), (gain_self, gain_cross, gain_ffn))
    wide = reduce_group(grads[11:13], (w_gate, w_up))
    thin = reduce_group(grads[1:5] + grads[6:10] + grads[13:14], narrow)
    return (
        (result_rows, grad_rows_dec, grad_rows_enc, gains[0])
        + tuple(thin[0:4])
        + (gains[1],)
        + tuple(thin[4:8])
        + (gains[2], *wide, thin[8])
    )


def solution(mesh):
    placed = (
        P(("dp", "fsdp"), None, None),
        P(("dp", "fsdp"), None, None),
        P(("dp", "fsdp"), None),
        P(("dp", "fsdp"), None),
        P(("dp", "fsdp"), None, None),
        P("fsdp"),
        P("fsdp", None),
        P("fsdp", None),
        P("fsdp", None),
        P("fsdp", None),
        P("fsdp"),
        P("fsdp", None),
        P("fsdp", None),
        P("fsdp", None),
        P("fsdp", None),
        P("fsdp"),
        P("fsdp", None),
        P("fsdp", None),
        P("fsdp", None),
    )
    return jax.shard_map(
        body,
        mesh=mesh,
        in_specs=placed,
        out_specs=(
            P(("dp", "fsdp"), None, None),
            P(("dp", "fsdp"), None, None),
            P(("dp", "fsdp"), None, None),
            P("fsdp"),
            P("fsdp", None),
            P("fsdp", None),
            P("fsdp", None),
            P("fsdp", None),
            P("fsdp"),
            P("fsdp", None),
            P("fsdp", None),
            P("fsdp", None),
            P("fsdp", None),
            P("fsdp"),
            P("fsdp", None),
            P("fsdp", None),
            P("fsdp", None),
        ),
        check_vma=False,
    )
```

profile of v0, /device:TPU:0, one launch (start us, length us, event | category | flops | bytes accessed | tf_op | source)
XLA Modules:
  0.0 545.3 jit_solution(10635128616492890739)
XLA Ops:
  7.3 2.2 pad_maximum_fusion.1
  17.5 16.0 %all-reduce = bf16[2304]{0:T(1024)(128)(2,1)S(1)} all-reduce(bf16[2304]{0:T(1024)(128)(2,1)S(1)} %dynamic-update-slice), channel_id=2, replica_groups=mesh['dp'=4,'fsdp'=8] {'fsdp'}, use_global_device_ids=true, to_apply=%add | all-reduce | flops 2304 | bytes 9216
  35.1 24.0 %all-gather.11.cloned.1.call-done = bf16[1536,2048]{1,0:T(8,128)(2,1)} async-done(((bf16[192,2048]{1,0:T(8,128)(2,1)}), bf16[1536,2048]{1,0:T(8,128)(2,1)}) %all-gather.11.cloned.1.call-update) | async-done | bytes 6291472 | tf_op jit(solution)/shard_map/all_gather | solution.py:96
  59.1 6.7 %fusion.43 = (bf16[8,96,2048]{2,1,0:T(8,128)(2,1)}, bf16[8,96,2048]{2,1,0:T(8,128)(2,1)}) fusion(bf16[8,192,2048]{2,1,0:T(8,128)(2,1)} %bitcast.212), kind=kLoop, calls=%fused_computation.149 | loop fusion | bytes 12582912 | tf_op jit(solution)/shard_map/slice | solution.py:100
  65.8 67.4 %all-gather.9.cloned.1.call-done = bf16[8192,768]{1,0:T(8,128)(2,1)} async-done(((bf16[1024,768]{1,0:T(8,128)(2,1)}), bf16[8192,768]{1,0:T(8,128)(2,1)}) %all-gather.9.cloned.1.call-update) | async-done | bytes 12582928 | tf_op jit(solution)/shard_map/all_gather | solution.py:96
  133.1 3.8 slice.125
  136.9 6.9 %fusion.42 = (bf16[8,96,768]{2,1,0:T(8,128)(2,1)}, bf16[8,96,768]{2,1,0:T(8,128)(2,1)}, bf16[8,96,768]{2,1,0:T(8,128)(2,1)}, bf16[8,96,768]{2,1,0:T(8,128)(2,1)}...) fusion(bf16[8,1024,768]{2,1,0:T(8,128)(2,1)} %bitcast.197), kind=kLoop, calls=%fused_computation.148 | loop fusion | bytes 18874368 | tf_op jit(solution)/shard_map/slice | solution.py:100
  145.8 2.7 convolution_convert_fusion.10
  148.5 1.3 copy.105
  149.8 3.2 convolution_convert_fusion.11
  153.0 2.2 copy.104
  155.2 3.9 convolution_convert_fusion.1
  159.2 2.6 convolution_convert_fusion.2
  167.7 1.5 convolution_convert_fusion.8
  169.1 2.2 copy.110
  171.3 3.5 fusion
  174.9 3.2 exponential_reduce_fusion
  178.3 2.6 convolution_convert_fusion.3
  181.8 1.3 copy-done.3
  187.1 4.7 multiply_convert_fusion.3
  191.7 1.4 fusion.48
  193.4 2.1 multiply_reduce_fusion.2
  195.9 1.4 convolution_convert_fusion.7
  197.3 1.9 bitcast_convert_fusion.3
  199.2 2.2 copy.113
  201.5 7.2 %convolution_convert_fusion = bf16[2,12,64,512]{3,2,1,0:T(8,128)(2,1)} fusion(bf16[2,176,12,64]{1,3,2,0:T(8,128)(2,1)} %bitcast.225, f32[2,12,176,512]{3,2,1,0:T(8,128)} %copy-done.1, f32[2,12,176]{2,1,0:T(8,128)} %copy-done.55, pred[2,176,512]{2,1,0:T(8,128)(4,1)} %broadcast_compare_fusion), kind=kOutput, calls=%fused_computation.46 | convolution fusion | flops 286261248 | bytes 10961408 | tf_op jit(solution)/shard_map/rhqk,rqhd->rkhd/dot_general | solution.py:69
  208.7 5.9 %multiply_reduce_fusion = (f32[2,12,176]{2,1,0:T(8,128)S(1)}, f32[2,12,176,512]{3,2,1,0:T(8,128)S(1)}) fusion(f32[2,12,176,512]{3,2,1,0:T(8,128)} %copy-done.1, f32[2,12,176]{2,1,0:T(8,128)S(1)} %copy-done.56, pred[2,176,512]{2,1,0:T(8,128)(4,1)S(1)} %copy-done.30, bf16[2,176,12,64]{1,3,2,0:T(8,128)(2,1)S(1)} %bitcast.226, ...), kind=kOutput, calls=%fused_computation.1 | convolution fusion | flops 287633280 | bytes 19629056 | tf_op jit(solution)/shard_map/rqhd,rkhd->rhqk/dot_general | solution.py:75
  214.7 2.7 multiply_convert_fusion
  217.5 1.5 multiply_convert_fusion.7
  219.0 2.1 multiply_convert_fusion.2
  221.1 1.5 multiply_reduce_fusion.3
  222.6 2.0 bitcast_convert_fusion.6
  225.9 1.4 convolution_convert_fusion.6
  227.4 1.9 bitcast_convert_fusion.7
  229.2 1.3 copy.115
  230.6 3.5 convolution_convert_fusion.4
  234.1 4.1 multiply_reduce_fusion.1
  238.3 1.3 multiply_convert_fusion.1
  241.0 1.4 copy-done.43
  242.4 1.5 bitcast_convert_fusion.4
  244.0 2.1 bitcast_convert_fusion.2
  247.5 1.5 bitcast_convert_fusion.5
  261.0 1.9 constant_dynamic-update-slice_fusion.9
  263.9 3.3 bitcast_convert_fusion
  267.2 1.8 bitcast_convert_fusion.1
  269.1 4.9 pad_maximum_fusion
  274.1 81.4 %reduce-scatter.5.cloned.1.call-done = bf16[1,1024,768]{2,1,0:T(8,128)(2,1)} async-done(((bf16[8,1024,768]{2,1,0:T(8,128)(2,1)}), bf16[1,1024,768]{2,1,0:T(8,128)(2,1)}) %reduce-scatter.5.cloned.1.call-update) | async-done | bytes 1572880 | tf_op jit(solution)/shard_map/reduce_scatter | solution.py:115
  355.5 64.9 %reduce-scatter.9.cloned.1.call-done = bf16[1,192,2048]{2,1,0:T(8,128)(2,1)} async-done(((bf16[8,192,2048]{2,1,0:T(8,128)(2,1)}), bf16[1,192,2048]{2,1,0:T(8,128)(2,1)}) %reduce-scatter.9.cloned.1.call-update) | async-done | bytes 786448 | tf_op jit(solution)/shard_map/reduce_scatter | solution.py:115
  422.2 2.2 fusion.49
  424.5 2.2 convolution_add_fusion.2
  426.7 1.9 fusion.15
  428.8 2.5 fusion.18
  431.3 26.7 %reduce-scatter.7.cloned.1.call-done = bf16[256,768]{1,0:T(8,128)(2,1)} async-done(((bf16[1024,768]{1,0:T(8,128)(2,1)}), bf16[256,768]{1,0:T(8,128)(2,1)}) %reduce-scatter.7.cloned.1.call-update) | async-done | bytes 393232 | tf_op jit(solution)/shard_map/reduce_scatter | solution.py:116
  458.1 13.7 %all-reduce.2 = bf16[8,288]{1,0:T(8,128)(2,1)S(1)} all-reduce(bf16[8,288]{1,0:T(8,128)(2,1)S(1)} %pad_maximum_fusion.2), channel_id=5, replica_groups=mesh['dp'=4,'fsdp'=8] {'fsdp'}, use_global_device_ids=true, to_apply=%region_15.16.clone | all-reduce | flops 2304 | bytes 9216
  472.5 10.3 %all-reduce.3 = bf16[288]{0:T(512)(128)(2,1)S(1)} all-reduce(bf16[288]{0:T(512)(128)(2,1)S(1)} %dynamic-slice_reduce_fusion), channel_id=6, replica_groups=mesh['dp'=4,'fsdp'=8] {'dp'}, use_global_device_ids=true, to_apply=%region_16.17.clone | all-reduce | flops 288 | bytes 1152
  483.1 8.6 %all-reduce.1 = bf16[288]{0:T(512)(128)(2,1)S(1)} all-reduce(bf16[288]{0:T(512)(128)(2,1)S(1)} %dynamic-update-slice.1), channel_id=1, replica_groups=mesh['dp'=4,'fsdp'=8] {'dp'}, use_global_device_ids=true, to_apply=%add.1 | all-reduce | flops 288 | bytes 1152
  492.3 3.3 fusion.50
  495.8 2.1 fusion.11
  497.9 3.1 convolution_add_fusion
  501.0 28.7 %all_gather.35 = bf16[192,2048]{1,0:T(8,128)(2,1)S(1)} all-gather(bf16[48,2048]{1,0:T(8,128)(2,1)} %reduce-scatter.11.cloned.1.call-done), channel_id=1, replica_groups=mesh['dp'=4,'fsdp'=8] {'dp'}, dimensions={0}, use_global_device_ids=true | all-gather | bytes 983040 | tf_op jit(solution)/shard_map/all_gather | solution.py:117
  529.7 1.3 slice_convert_fusion.1
  531.1 2.4 all-gather.7.cloned.1.call-done
  533.5 1.9 slice_convert_fusion
  535.4 2.8 slice_convert_fusion.3
  (255 shorter events, 41.9 us)
Async XLA Ops:
  7.2 148.0 %copy-start = (bf16[2,512,768]{2,1,0:T(8,128)(2,1)S(1)}, bf16[2,512,768]{2,1,0:T(8,128)(2,1)}, u32[]{:S(2)}) copy-start(bf16[2,512,768]{2,1,0:T(8,128)(2,1)} %param.20) | copy-start | bytes 4718596
  7.2 2.4 copy-start.57
  7.2 3.1 copy-start.58
  7.2 3.7 copy-start.59
  7.2 4.4 copy-start.60
  7.2 5.1 copy-start.61
  7.3 5.7 %copy-start.62 = (bf16[96,768]{1,0:T(8,128)(2,1)S(1)}, bf16[96,768]{1,0:T(8,128)(2,1)}, u32[]{:S(2)}) copy-start(bf16[96,768]{1,0:T(8,128)(2,1)} %param.31) | copy-start | bytes 442372
  7.3 51.8 %all-gather.11.cloned.1.call-start = ((), (), s32[]{:S(2)}) async-start(), calls=%async_computation.10 | async-start | bytes 7077888 | tf_op jit(solution)/shard_map/all_gather | solution.py:96
  9.5 4.1 copy-start.63
  9.5 4.8 copy-start.64
  9.5 5.5 %copy-start.52 = (bf16[256,768]{1,0:T(8,128)(2,1)S(1)}, bf16[256,768]{1,0:T(8,128)(2,1)}, u32[]{:S(2)}) copy-start(bf16[256,768]{1,0:T(8,128)(2,1)} %param.37) | copy-start | bytes 1179652
  9.6 123.6 %all-gather.9.cloned.1.call-start = ((), (), s32[]{:S(2)}) async-start(), calls=%async_computation.9 | async-start | bytes 14155776 | tf_op jit(solution)/shard_map/all_gather | solution.py:96
  13.0 2.9 copy-start.70
  13.0 2.9 copy-start.71
  13.0 4.2 copy-start.73
  13.0 4.2 copy-start.74
  13.0 4.2 copy-start.75
  13.7 20.2 %copy-start.20 = (bf16[2,176,768]{2,1,0:T(8,128)(2,1)S(1)}, bf16[2,176,768]{2,1,0:T(8,128)(2,1)}, u32[]{:S(2)}) copy-start(bf16[2,176,768]{2,1,0:T(8,128)(2,1)} %param.19) | copy-start | bytes 1622020
  15.0 19.0 %copy-start.65 = (s32[2,176]{1,0:T(2,128)S(1)}, s32[2,176]{1,0:T(2,128)}, u32[]{:S(2)}) copy-start(s32[2,176]{1,0:T(2,128)} %param.21) | copy-start | bytes 4228
  15.0 19.2 %copy-start.69 = (s32[2,512]{1,0:T(2,128)S(1)}, s32[2,512]{1,0:T(2,128)}, u32[]{:S(2)}) copy-start(s32[2,512]{1,0:T(2,128)} %param.22) | copy-start | bytes 12292
  15.8 339.6 %reduce-scatter.5.cloned.1.call-start = ((), (), s32[]{:S(2)}) async-start(), calls=%async_computation.4 | async-start | bytes 14155776 | tf_op jit(solution)/shard_map/reduce_scatter | solution.py:115
  149.8 11.9 %copy-start.14 = (bf16[2,176,768]{1,2,0:T(8,128)(2,1)}, bf16[2,176,768]{1,2,0:T(8,128)(2,1)S(1)}, u32[]{:S(2)}) copy-start(bf16[2,176,768]{1,2,0:T(8,128)(2,1)S(1)} %copy.105) | copy-start | bytes 1622020
  155.2 3.9 copy-start.23
  162.7 2.1 copy-start.2
  162.7 2.1 copy-start.34
  163.8 2.3 copy-start.53
  171.3 3.5 copy-start.29
  174.8 3.4 copy-start.1
  174.8 3.4 copy-start.40
  178.1 2.8 copy-start.55
  178.3 2.6 copy-start.7
  180.9 2.3 copy-start.3
  181.6 13.9 %copy-start.8 = (f32[2,176,768]{2,1,0:T(8,128)}, f32[2,176,768]{2,1,0:T(8,128)S(1)}, u32[]{:S(2)}) copy-start(f32[2,176,768]{2,1,0:T(8,128)S(1)} %get-tuple-element.63) | copy-start | bytes 3244036
  181.8 2.6 copy-start.18
  201.4 7.3 %copy-start.30 = (pred[2,176,512]{2,1,0:T(8,128)(4,1)S(1)}, pred[2,176,512]{2,1,0:T(8,128)(4,1)}, u32[]{:S(2)}) copy-start(pred[2,176,512]{2,1,0:T(8,128)(4,1)} %broadcast_compare_fusion) | copy-start | bytes 540676
  201.4 7.3 %copy-start.31 = (bf16[2,176,768]{1,2,0:T(8,128)(2,1)S(1)}, bf16[2,176,768]{1,2,0:T(8,128)(2,1)}, u32[]{:S(2)}) copy-start(bf16[2,176,768]{1,2,0:T(8,128)(2,1)} %copy.113) | copy-start | bytes 1622020
  201.4 7.3 %copy-start.41 = (bf16[768,2,512]{2,0,1:T(8,128)(2,1)S(1)}, bf16[768,2,512]{2,0,1:T(8,128)(2,1)}, u32[]{:S(2)}) copy-start(bf16[768,2,512]{2,0,1:T(8,128)(2,1)} %convolution_convert_fusion.2) | copy-start | bytes 4718596
  201.4 7.3 %copy-start.56 = (f32[2,12,176]{2,1,0:T(8,128)S(1)}, f32[2,12,176]{2,1,0:T(8,128)}, u32[]{:S(2)}) copy-start(f32[2,12,176]{2,1,0:T(8,128)} %copy-done.55) | copy-start | bytes 50692
  201.4 13.2 %slice-start = ((s8[8650752]{0:T(1024)(128)(4,1)}), s8[4194304]{0:T(1024)(128)(4,1)S(1)}, s32[]{:S(2)}) async-start(s8[8650752]{0:T(1024)(128)(4,1)} %bitcast.192), calls=%async_computation.11 | async-start | bytes 8388608
  201.5 13.2 %slice-start.1 = ((s8[8650752]{0:T(1024)(128)(4,1)}), s8[4194304]{0:T(1024)(128)(4,1)S(1)}, s32[]{:S(2)}) async-start(s8[8650752]{0:T(1024)(128)(4,1)} %bitcast.192), calls=%async_computation.12 | async-start | bytes 8388608
  208.7 6.0 %slice-start.2 = ((s8[8650752]{0:T(1024)(128)(4,1)}), s8[262144]{0:T(1024)(128)(4,1)S(1)}, s32[]{:S(2)}) async-start(s8[8650752]{0:T(1024)(128)(4,1)} %bitcast.192), calls=%async_computation.13 | async-start | bytes 524288
  214.7 2.7 copy-start.17
  227.4 3.2 copy-start.54
  230.6 3.5 copy-start.35
  230.6 7.7 %slice-start.3 = ((s8[4325376]{0:T(1024)(128)(4,1)}), s8[4194304]{0:T(1024)(128)(4,1)S(1)}, s32[]{:S(2)}) async-start(s8[4325376]{0:T(1024)(128)(4,1)} %bitcast.194), calls=%async_computation.14 | async-start | bytes 8388608
  234.1 11.9 %copy-start.48 = (bf16[2,12,64,176]{3,2,1,0:T(8,128)(2,1)}, bf16[2,12,64,176]{3,2,1,0:T(8,128)(2,1)S(1)}, u32[]{:S(2)}) copy-start(bf16[2,12,64,176]{3,2,1,0:T(8,128)(2,1)S(1)} %convolution_convert_fusion.4) | copy-start | bytes 1622020
  234.1 4.1 slice-start.4
  240.5 8.5 %copy-start.38 = (bf16[2,12,64,176]{3,2,1,0:T(8,128)(2,1)}, bf16[2,12,64,176]{3,2,1,0:T(8,128)(2,1)S(1)}, u32[]{:S(2)}) copy-start(bf16[2,12,64,176]{3,2,1,0:T(8,128)(2,1)S(1)} %multiply_convert_fusion.5) | copy-start | bytes 1622020
  241.0 8.9 %copy-start.36 = (bf16[2,12,64,176]{3,2,1,0:T(8,128)(2,1)}, bf16[2,12,64,176]{3,2,1,0:T(8,128)(2,1)S(1)}, u32[]{:S(2)}) copy-start(bf16[2,12,64,176]{3,2,1,0:T(8,128)(2,1)S(1)} %multiply_convert_fusion.6) | copy-start | bytes 1622020
  262.9 157.5 %reduce-scatter.9.cloned.1.call-start = ((), (), s32[]{:S(2)}) async-start(), calls=%async_computation.7 | async-start | bytes 7077888 | tf_op jit(solution)/shard_map/reduce_scatter | solution.py:115
  263.9 3.3 copy-start.82
  274.0 148.0 %copy-start.72 = (bf16[768]{0:T(1024)(128)(2,1)S(1)}, bf16[768]{0:T(1024)(128)(2,1)}, u32[]{:S(2)}) copy-start(bf16[768]{0:T(1024)(128)(2,1)} %get-tuple-element.19) | copy-start | bytes 4612
  274.0 148.1 %copy-start.66 = (bf16[768]{0:T(1024)(128)(2,1)S(1)}, bf16[768]{0:T(1024)(128)(2,1)}, u32[]{:S(2)}) copy-start(bf16[768]{0:T(1024)(128)(2,1)} %get-tuple-element.17) | copy-start | bytes 4612
  274.0 148.2 %copy-start.37 = (bf16[2,12,64,176]{3,2,1,0:T(8,128)(2,1)S(1)}, bf16[2,12,64,176]{3,2,1,0:T(8,128)(2,1)}, u32[]{:S(2)}) copy-start(bf16[2,12,64,176]{3,2,1,0:T(8,128)(2,1)} %copy-done.36) | copy-start | bytes 1622020
  274.0 184.0 %reduce-scatter.7.cloned.1.call-start = ((), (), s32[]{:S(2)}) async-start(), calls=%async_computation.5 | async-start | bytes 1966080 | tf_op jit(solution)/shard_map/reduce_scatter | solution.py:116
  355.5 145.5 %reduce-scatter.11.cloned.1.call-start = ((), (), s32[]{:S(2)}) async-start(), calls=%async_computation.8 | async-start | bytes 983040 | tf_op jit(solution)/shard_map/reduce_scatter | solution.py:116
  420.5 113.0 %all-gather.7.cloned.1.call-start = ((), (), s32[]{:S(2)}) async-start(), calls=%async_computation.6 | async-start | bytes 1966080 | tf_op jit(solution)/shard_map/all_gather | solution.py:117
  422.2 2.2 copy-start.39
  424.4 2.3 copy-start.25
  424.4 2.3 copy-start.49
  492.3 3.3 copy-start.9
  492.3 3.3 copy-start.33
  492.3 3.5 copy-start.80
  495.8 2.1 copy-start.44
  (31 other events, 48.9 us)
Sparse Core Ops, SparseCore 0:
  10.6 48.4 all-gather.10
  61.0 72.1 all-gather.8
  263.0 92.3 reduce-scatter.4
  358.7 61.7 reduce-scatter.8
  422.7 35.2 reduce-scatter.6
  460.3 22.3 reduce-scatter.10
  484.3 49.0 all-gather.6
where the time goes:
time: 549 us; the launch traced here: 545 us
  waiting for transfers between devices  267 us (49%)
  matrix products  98.7 us (18%)
  blocking collectives  77.3 us (14%)
  local copies, waits for them, and re-layouts  57.7 us (11%)
  other arithmetic  26.8 us (5%)
  between operations  17.4 us (3%)
    reduce_scatter x2, waiting for transfers between devices, reduce_group(): owned = lax.psum_scatter(joined, 'fsdp', scatter_dimension=0, tiled=False)  146 us
    all_gather x2, waiting for transfers between devices, gather_group(): whole = lax.all_gather(joined, 'fsdp', axis=0, tiled=False)  91.4 us
    unnamed x4, blocking collectives  48.6 us
    all_gather x1, blocking collectives, reduce_group(): summed = lax.all_gather(quarter, 'dp', axis=0, tiled=True)  28.7 us
    unnamed x198, local copies, waits for them, and re-layouts  26.9 us
    reduce_scatter x2, waiting for transfers between devices, reduce_group(): quarter = lax.psum_scatter(owned, 'dp', scatter_dimension=0, tiled=True)  26.7 us
    dot_general x11, matrix products, input_grad(): jnp.einsum('rln,dn->rld', grad_out, weight, preferred_element_type=jnp.fl...  25.4 us
    dot_general x11, matrix products, project(): jnp.einsum('rld,dn->rln', acts, weight, preferred_element_type=jnp.float32)  20.7 us
  transfers between devices with their start and end apart: 7, of which 6 were waited for; matrix products, arithmetic and copies ran while one was open for 8% of the time, Pallas kernels for 0%

commit v1 on v0

--- a/solution.py
+++ b/solution.py
@@ -114,7 +114,14 @@
     )
     owned = lax.psum_scatter(joined, "fsdp", scatter_dimension=0, tiled=False)
     quarter = lax.psum_scatter(owned, "dp", scatter_dimension=0, tiled=True)
-    summed = lax.all_gather(quarter, "dp", axis=0, tiled=True)
+    ways, here, hop = (lax.axis_size("dp"), lax.axis_index("dp"), quarter.shape[0])
+    line, have = (quarter, 1)
+    while have < ways:
+        line = jnp.concatenate(
+            [line, lax.ppermute(line, "dp", [(d, (d - have) % ways) for d in range(ways)])], axis=0
+        )
+        have = 2 * have
+    summed = jnp.roll(line, here * hop, axis=0)
     parts = []
     start = 0
     for shard in shards:

time: 549 us -> 520 us (0.947)
  blocking collectives: 77.3 us -> 41 us
  waiting for transfers between devices: 267 us -> 254 us
  starting transfers between devices: 0.53 us -> 13.1 us
  local copies, waits for them, and re-layouts: 57.7 us -> 69 us
  matrix products: 98.7 us -> 93.2 us
    ppermute x0 -> x6, waiting for transfers between devices: none -> 63.2 us  [reduce_group(): lax.ppermute(line, 'dp', [(d, (d - have) % ways) for d in range(ways)])]
    reduce_scatter x2, waiting for transfers between devices: 146 us -> 93.9 us  [reduce_group(): owned = lax.psum_scatter(joined, 'fsdp', scatter_dimension=0, tiled=False)]
    all_gather x1 -> x0, blocking collectives: 28.7 us -> none  [reduce_group(): summed = lax.all_gather(quarter, 'dp', axis=0, tiled=True)]
    reduce_scatter x2, waiting for transfers between devices: 26.7 us -> 5.89 us  [reduce_group(): quarter = lax.psum_scatter(owned, 'dp', scatter_dimension=0, tiled=True)]
    ppermute x0 -> x6, starting transfers between devices: none -> 12.9 us  [reduce_group(): lax.ppermute(line, 'dp', [(d, (d - have) % ways) for d in range(ways)])]
    unnamed x198 -> x225, local copies, waits for them, and re-layouts: 26.9 us -> 35.2 us
    unnamed x4 -> x3, blocking collectives: 48.6 us -> 41 us
    dot_general x2, matrix products: 10.7 us -> 3.76 us  [attend_backward(): jnp.einsum('rhqk,rqhd->rkhd', weights_full.astype(jnp.bfloat16), grad_hea...]
  transfers between devices with their start and end apart: 7 -> 12, of which waited for: 6 -> 10; matrix products, arithmetic and copies ran while one was open for 8% -> 18% of each run, Pallas kernels for 0% -> 0%
where the time goes in v1:
time: 520 us; the launch traced here: 516 us
  waiting for transfers between devices  254 us (49%)
  matrix products  93.2 us (18%)
  local copies, waits for them, and re-layouts  69 us (13%)
  blocking collectives  41 us (8%)
  other arithmetic  28.1 us (5%)
  between operations  17 us (3%)
  starting transfers between devices  13.1 us (3%)
    reduce_scatter x2, waiting for transfers between devices, reduce_group(): owned = lax.psum_scatter(joined, 'fsdp', scatter_dimension=0, tiled=False)  93.9 us
    all_gather x2, waiting for transfers between devices, gather_group(): whole = lax.all_gather(joined, 'fsdp', axis=0, tiled=False)  91.3 us
    ppermute x6, waiting for transfers between devices, reduce_group(): lax.ppermute(line, 'dp', [(d, (d - have) % ways) for d in range(ways)])  63.2 us
    unnamed x3, blocking collectives  41 us
    unnamed x225, local copies, waits for them, and re-layouts  35.2 us
    dot_general x11, matrix products, input_grad(): jnp.einsum('rln,dn->rld', grad_out, weight, preferred_element_type=jnp.fl...  26.5 us
    dot_general x11, matrix products, project(): jnp.einsum('rld,dn->rln', acts, weight, preferred_element_type=jnp.float32)  21.6 us
    slice x3, local copies, waits for them, and re-layouts, gather_group(): part = whole[:, start:start + shard.shape[0]]  17.4 us
  transfers between devices with their start and end apart: 12, of which 10 were waited for; matrix products, arithmetic and copies ran while one was open for 18% of the time, Pallas kernels for 0%

profile of v1, /device:TPU:0, one launch (start us, length us, event | category | flops | bytes accessed | tf_op | source)
XLA Modules:
  0.0 515.8 jit_solution(14804895855744150378)
XLA Ops:
  7.3 2.2 pad_maximum_fusion.1
  17.5 15.9 %all-reduce = bf16[2304]{0:T(1024)(128)(2,1)S(1)} all-reduce(bf16[2304]{0:T(1024)(128)(2,1)S(1)} %dynamic-update-slice), channel_id=2, replica_groups=mesh['dp'=4,'fsdp'=8] {'fsdp'}, use_global_device_ids=true, to_apply=%add | all-reduce | flops 2304 | bytes 9216
  35.1 24.0 %all-gather.8.cloned.1.call-done = bf16[1536,2048]{1,0:T(8,128)(2,1)} async-done(((bf16[192,2048]{1,0:T(8,128)(2,1)}), bf16[1536,2048]{1,0:T(8,128)(2,1)}) %all-gather.8.cloned.1.call-update) | async-done | bytes 6291472 | tf_op jit(solution)/shard_map/all_gather | solution.py:96
  59.1 6.8 %fusion.43 = (bf16[8,96,2048]{2,1,0:T(8,128)(2,1)}, bf16[8,96,2048]{2,1,0:T(8,128)(2,1)}) fusion(bf16[8,192,2048]{2,1,0:T(8,128)(2,1)} %bitcast.215), kind=kLoop, calls=%fused_computation.164 | loop fusion | bytes 12582912 | tf_op jit(solution)/shard_map/slice | solution.py:100
  65.8 67.3 %all-gather.6.cloned.1.call-done = bf16[8192,768]{1,0:T(8,128)(2,1)} async-done(((bf16[1024,768]{1,0:T(8,128)(2,1)}), bf16[8192,768]{1,0:T(8,128)(2,1)}) %all-gather.6.cloned.1.call-update) | async-done | bytes 12582928 | tf_op jit(solution)/shard_map/all_gather | solution.py:96
  133.1 3.7 slice.125
  136.9 7.0 %fusion.42 = (bf16[8,96,768]{2,1,0:T(8,128)(2,1)}, bf16[8,96,768]{2,1,0:T(8,128)(2,1)}, bf16[8,96,768]{2,1,0:T(8,128)(2,1)}, bf16[8,96,768]{2,1,0:T(8,128)(2,1)}...) fusion(bf16[8,1024,768]{2,1,0:T(8,128)(2,1)} %bitcast.200), kind=kLoop, calls=%fused_computation.163 | loop fusion | bytes 18874368 | tf_op jit(solution)/shard_map/slice | solution.py:100
  144.8 1.4 convolution_convert_fusion.9
  146.3 1.3 copy.106
  147.6 3.0 convolution_convert_fusion.10
  150.6 1.3 copy.105
  151.9 2.9 convolution_convert_fusion.11
  154.8 2.2 copy.104
  157.0 4.0 convolution_convert_fusion.1
  161.0 2.6 convolution_convert_fusion.2
  169.4 1.5 convolution_convert_fusion.8
  170.8 2.2 copy.110
  173.0 3.5 fusion
  176.6 3.2 exponential_reduce_fusion
  180.0 2.6 convolution_convert_fusion.3
  183.6 1.5 copy-done.4
  189.0 4.7 multiply_convert_fusion.3
  193.7 1.4 fusion.47
  195.1 3.5 bitcast_convert_fusion.1
  198.6 3.5 bitcast_convert_fusion
  202.1 2.1 multiply_reduce_fusion.2
  205.6 1.4 convolution_convert_fusion.7
  207.1 2.2 copy.113
  209.3 6.6 %pad_maximum_fusion = bf16[8,192,2048]{2,1,0:T(8,128)(2,1)} fusion(bf16[8,96,2048]{2,1,0:T(8,128)(2,1)} %bitcast.242, bf16[8,96,2048]{2,1,0:T(8,128)(2,1)} %bitcast.241), kind=kLoop, calls=%fused_computation.6 | loop fusion | flops 12582912 | bytes 12582912 | tf_op jit(solution)/shard_map/concatenate | solution.py:108
  215.9 7.7 %multiply_reduce_fusion = (f32[2,12,176]{2,1,0:T(8,128)S(1)}, f32[2,12,176,512]{3,2,1,0:T(8,128)S(1)}) fusion(f32[2,12,176,512]{3,2,1,0:T(8,128)} %copy-done.1, f32[2,12,176]{2,1,0:T(8,128)} %copy-done.59, pred[2,176,512]{2,1,0:T(8,128)(4,1)} %broadcast_compare_fusion, bf16[2,176,12,64]{1,3,2,0:T(8,128)(2,1)} %bitcast.228, bf16[2,512,12,64]{1,3,2,0:T(8,128)(2,1)} %bitcast.245), kind=kOutput, calls=%fused_computation.1 | convolution fusion | flops 287633280 | bytes 19629056 | tf_op jit(solution)/shard_map/rqhd,rkhd->rhqk/dot_general | solution.py:75
  223.7 2.7 multiply_convert_fusion
  226.5 1.5 multiply_convert_fusion.7
  228.8 1.5 multiply_reduce_fusion.3
  231.9 1.4 convolution_convert_fusion.6
  233.3 2.2 copy.115
  235.5 4.4 multiply_reduce_fusion.1
  240.0 1.4 multiply_convert_fusion.1
  257.6 1.4 bitcast_convert_fusion.5
  261.6 2.6 convolution_convert_fusion
  264.3 1.4 bitcast_convert_fusion.4
  270.4 1.8 bitcast_convert_fusion.2
  272.3 1.9 constant_dynamic-update-slice_fusion.9
  274.2 3.5 reduce-scatter.9.cloned.1.call-done
  280.3 3.2 convolution_add_fusion.2
  283.5 90.4 %reduce-scatter.5.cloned.1.call-done = bf16[1,1024,768]{2,1,0:T(8,128)(2,1)} async-done(((bf16[8,1024,768]{2,1,0:T(8,128)(2,1)}), bf16[1,1024,768]{2,1,0:T(8,128)(2,1)}) %reduce-scatter.5.cloned.1.call-update) | async-done | bytes 1572880 | tf_op jit(solution)/shard_map/reduce_scatter | solution.py:115
  374.0 3.4 fusion.15
  377.7 13.4 %all-reduce.1 = bf16[8,288]{1,0:T(8,128)(2,1)S(1)} all-reduce(bf16[8,288]{1,0:T(8,128)(2,1)S(1)} %pad_maximum_fusion.4), channel_id=5, replica_groups=mesh['dp'=4,'fsdp'=8] {'fsdp'}, use_global_device_ids=true, to_apply=%region_15.16.clone | all-reduce | flops 2304 | bytes 9216
  391.8 11.7 %all-reduce.2 = bf16[288]{0:T(512)(128)(2,1)S(1)} all-reduce(bf16[288]{0:T(512)(128)(2,1)S(1)} %dynamic-slice_reduce_fusion), channel_id=6, replica_groups=mesh['dp'=4,'fsdp'=8] {'dp'}, use_global_device_ids=true, to_apply=%region_16.17.clone | all-reduce | flops 288 | bytes 1152
  403.8 3.3 fusion.49
  407.2 2.1 fusion.11
  409.3 3.1 convolution_add_fusion
  414.2 2.8 collective-permute-done.1
  417.2 1.3 collective-permute-start.4
  419.1 14.5 %collective-permute-done.4 = bf16[48,2048]{1,0:T(8,128)(2,1)S(1)} collective-permute-done((bf16[48,2048]{1,0:T(8,128)(2,1)}, bf16[48,2048]{1,0:T(8,128)(2,1)S(1)}, u32[]{:S(2)}, u32[]{:S(2)}) %collective-permute-start.4) | collective-permute-done | bytes 196640 | tf_op jit(solution)/shard_map/ppermute | solution.py:121
  434.6 1.8 collective-permute-start.5
  436.4 1.6 constant_dynamic-update-slice_fusion.29
  438.7 5.9 %reduce-scatter.7.cloned.1.call-done = bf16[256,768]{1,0:T(8,128)(2,1)} async-done(((bf16[1024,768]{1,0:T(8,128)(2,1)}), bf16[256,768]{1,0:T(8,128)(2,1)}) %reduce-scatter.7.cloned.1.call-update) | async-done | bytes 393232 | tf_op jit(solution)/shard_map/reduce_scatter | solution.py:116
  444.6 2.4 collective-permute-start.2
  447.0 9.7 %collective-permute-done.5 = bf16[96,2048]{1,0:T(8,128)(2,1)S(1)} collective-permute-done((bf16[96,2048]{1,0:T(8,128)(2,1)S(1)}, bf16[96,2048]{1,0:T(8,128)(2,1)S(1)}, u32[]{:S(2)}, u32[]{:S(2)}) %collective-permute-start.5) | collective-permute-done | bytes 393248 | tf_op jit(solution)/shard_map/ppermute | solution.py:121
  458.2 7.2 %collective-permute-done.2 = bf16[256,768]{1,0:T(8,128)(2,1)S(1)} collective-permute-done((bf16[256,768]{1,0:T(8,128)(2,1)}, bf16[256,768]{1,0:T(8,128)(2,1)S(1)}, u32[]{:S(2)}, u32[]{:S(2)}) %collective-permute-start.2) | collective-permute-done | bytes 393248 | tf_op jit(solution)/shard_map/ppermute | solution.py:121
  466.4 6.7 %collective-permute-start.3 = (bf16[512,768]{1,0:T(8,128)(2,1)S(1)}, bf16[512,768]{1,0:T(8,128)(2,1)S(1)}, u32[]{:S(2)}, u32[]{:S(2)}) collective-permute-start(bf16[512,768]{1,0:T(8,128)(2,1)S(1)} %pad_maximum_fusion.2), channel_id=1, source_target_pairs={{0,16},{8,24},{16,0},{24,8},{1,17},{9,25},{17,1},{25,9},{2,18},{10... | collective-permute-start | bytes 2359304 | tf_op jit(solution)/shard_map/ppermute | solution.py:121
  474.5 2.5 dynamic-slice_convert_fusion.1
  477.0 29.1 %collective-permute-done.3 = bf16[512,768]{1,0:T(8,128)(2,1)S(1)} collective-permute-done((bf16[512,768]{1,0:T(8,128)(2,1)S(1)}, bf16[512,768]{1,0:T(8,128)(2,1)S(1)}, u32[]{:S(2)}, u32[]{:S(2)}) %collective-permute-start.3) | collective-permute-done | bytes 786464 | tf_op jit(solution)/shard_map/ppermute | solution.py:121
  507.3 1.4 dynamic-slice_convert_fusion.3
  (298 shorter events, 60.3 us)
Async XLA Ops:
  7.2 149.8 %copy-start = (bf16[2,512,768]{2,1,0:T(8,128)(2,1)S(1)}, bf16[2,512,768]{2,1,0:T(8,128)(2,1)}, u32[]{:S(2)}) copy-start(bf16[2,512,768]{2,1,0:T(8,128)(2,1)} %param.20) | copy-start | bytes 4718596
  7.2 3.1 copy-start.65
  7.2 3.7 copy-start.66
  7.2 4.4 copy-start.67
  7.2 5.1 copy-start.68
  7.3 5.7 %copy-start.69 = (bf16[96,768]{1,0:T(8,128)(2,1)S(1)}, bf16[96,768]{1,0:T(8,128)(2,1)}, u32[]{:S(2)}) copy-start(bf16[96,768]{1,0:T(8,128)(2,1)} %param.31) | copy-start | bytes 442372
  7.3 51.8 %all-gather.8.cloned.1.call-start = ((), (), s32[]{:S(2)}) async-start(), calls=%async_computation.9 | async-start | bytes 7077888 | tf_op jit(solution)/shard_map/all_gather | solution.py:96
  9.5 4.2 copy-start.70
  9.5 4.8 copy-start.71
  9.5 5.5 %copy-start.58 = (bf16[256,768]{1,0:T(8,128)(2,1)S(1)}, bf16[256,768]{1,0:T(8,128)(2,1)}, u32[]{:S(2)}) copy-start(bf16[256,768]{1,0:T(8,128)(2,1)} %param.37) | copy-start | bytes 1179652
  9.6 123.6 %all-gather.6.cloned.1.call-start = ((), (), s32[]{:S(2)}) async-start(), calls=%async_computation.8 | async-start | bytes 14155776 | tf_op jit(solution)/shard_map/all_gather | solution.py:96
  13.0 3.0 copy-start.77
  13.0 4.2 copy-start.79
  13.0 4.2 copy-start.80
  13.0 4.2 copy-start.81
  13.7 20.2 %copy-start.21 = (bf16[2,176,768]{2,1,0:T(8,128)(2,1)S(1)}, bf16[2,176,768]{2,1,0:T(8,128)(2,1)}, u32[]{:S(2)}) copy-start(bf16[2,176,768]{2,1,0:T(8,128)(2,1)} %param.19) | copy-start | bytes 1622020
  15.1 19.0 %copy-start.72 = (s32[2,176]{1,0:T(2,128)S(1)}, s32[2,176]{1,0:T(2,128)}, u32[]{:S(2)}) copy-start(s32[2,176]{1,0:T(2,128)} %param.21) | copy-start | bytes 4228
  15.1 19.2 %copy-start.76 = (s32[2,512]{1,0:T(2,128)S(1)}, s32[2,512]{1,0:T(2,128)}, u32[]{:S(2)}) copy-start(s32[2,512]{1,0:T(2,128)} %param.22) | copy-start | bytes 12292
  15.9 261.8 %reduce-scatter.9.cloned.1.call-start = ((), (), s32[]{:S(2)}) async-start(), calls=%async_computation.6 | async-start | bytes 7077888 | tf_op jit(solution)/shard_map/reduce_scatter | solution.py:115
  147.6 16.0 %copy-start.17 = (bf16[2,176,768]{1,2,0:T(8,128)(2,1)}, bf16[2,176,768]{1,2,0:T(8,128)(2,1)S(1)}, u32[]{:S(2)}) copy-start(bf16[2,176,768]{1,2,0:T(8,128)(2,1)S(1)} %copy.106) | copy-start | bytes 1622020
  157.0 4.0 copy-start.25
  173.0 3.5 copy-start.32
  176.5 3.4 copy-start.1
  176.5 3.4 copy-start.49
  179.7 2.8 copy-start.59
  180.0 2.6 copy-start.8
  183.4 20.8 %copy-start.9 = (f32[2,176,768]{2,1,0:T(8,128)}, f32[2,176,768]{2,1,0:T(8,128)S(1)}, u32[]{:S(2)}) copy-start(f32[2,176,768]{2,1,0:T(8,128)S(1)} %get-tuple-element.61) | copy-start | bytes 3244036
  215.8 158.1 %reduce-scatter.5.cloned.1.call-start = ((), (), s32[]{:S(2)}) async-start(), calls=%async_computation.4 | async-start | bytes 14155776 | tf_op jit(solution)/shard_map/reduce_scatter | solution.py:115
  215.9 7.8 %slice-start = ((s8[8650752]{0:T(1024)(128)(4,1)}), s8[4194304]{0:T(1024)(128)(4,1)S(1)}, s32[]{:S(2)}) async-start(s8[8650752]{0:T(1024)(128)(4,1)} %bitcast.191), calls=%async_computation.10 | async-start | bytes 8388608
  215.9 7.8 %slice-start.1 = ((s8[8650752]{0:T(1024)(128)(4,1)}), s8[4194304]{0:T(1024)(128)(4,1)S(1)}, s32[]{:S(2)}) async-start(s8[8650752]{0:T(1024)(128)(4,1)} %bitcast.191), calls=%async_computation.11 | async-start | bytes 8388608
  215.9 7.8 %slice-start.2 = ((s8[8650752]{0:T(1024)(128)(4,1)}), s8[262144]{0:T(1024)(128)(4,1)S(1)}, s32[]{:S(2)}) async-start(s8[8650752]{0:T(1024)(128)(4,1)} %bitcast.191), calls=%async_computation.12 | async-start | bytes 524288
  215.9 7.8 %copy-start.33 = (pred[2,176,512]{2,1,0:T(8,128)(4,1)S(1)}, pred[2,176,512]{2,1,0:T(8,128)(4,1)}, u32[]{:S(2)}) copy-start(pred[2,176,512]{2,1,0:T(8,128)(4,1)} %broadcast_compare_fusion) | copy-start | bytes 540676
  215.9 7.8 %copy-start.60 = (f32[2,12,176]{2,1,0:T(8,128)S(1)}, f32[2,12,176]{2,1,0:T(8,128)}, u32[]{:S(2)}) copy-start(f32[2,12,176]{2,1,0:T(8,128)} %copy-done.59) | copy-start | bytes 50692
  223.7 2.7 copy-start.20
  235.5 4.4 slice-start.6
  235.5 4.4 slice-start.7
  235.5 4.4 copy-start.63
  249.9 6.4 %slice-start.8 = ((s8[4325376]{0:T(1024)(128)(4,1)}), s8[4194304]{0:T(1024)(128)(4,1)S(1)}, s32[]{:S(2)}) async-start(s8[4325376]{0:T(1024)(128)(4,1)} %bitcast.197), calls=%async_computation.18 | async-start | bytes 8388608
  252.6 3.7 slice-start.9
  256.6 3.5 slice-start.3
  256.6 4.5 slice-start.4
  257.6 3.6 slice-start.5
  274.2 3.7 copy-start.84
  274.2 5.0 copy-start.29
  274.2 5.0 copy-start.43
  274.2 143.0 %reduce-scatter.11.cloned.1.call-start = ((), (), s32[]{:S(2)}) async-start(), calls=%async_computation.7 | async-start | bytes 983040 | tf_op jit(solution)/shard_map/reduce_scatter | solution.py:116
  277.8 166.8 %reduce-scatter.7.cloned.1.call-start = ((), (), s32[]{:S(2)}) async-start(), calls=%async_computation.5 | async-start | bytes 1966080 | tf_op jit(solution)/shard_map/reduce_scatter | solution.py:116
  280.3 93.7 %copy-start.27 = (bf16[8,96,768]{2,1,0:T(8,128)(2,1)S(1)}, bf16[8,96,768]{2,1,0:T(8,128)(2,1)}, u32[]{:S(2)}) copy-start(bf16[8,96,768]{2,1,0:T(8,128)(2,1)} %get-tuple-element.30) | copy-start | bytes 3538948
  283.5 90.5 %copy-start.24 = (bf16[2,176,768]{2,1,0:T(8,128)(2,1)S(1)}, bf16[2,176,768]{2,1,0:T(8,128)(2,1)}, u32[]{:S(2)}) copy-start(bf16[2,176,768]{2,1,0:T(8,128)(2,1)} %param.19) | copy-start | bytes 1622020
  374.0 3.4 copy-start.78
  374.0 3.5 copy-start.73
  403.5 3.6 copy-start.10
  403.5 3.6 copy-start.41
  403.6 3.6 copy-start.86
  403.6 8.9 %collective-permute-start = (bf16[72]{0:T(256)(128)(2,1)S(1)}, bf16[72]{0:T(256)(128)(2,1)S(1)}, u32[]{:S(2)}, u32[]{:S(2)}) collective-permute-start(bf16[72]{0:T(256)(128)(2,1)S(1)} %dynamic-slice.4), channel_id=1, source_target_pairs={{0,24},{8,0},{16,8},{24,16},{1,25},{9,1},{17,9},{25,17},{2,26},{10... | collective-permute-start | bytes 440 | tf_op jit(solution)/shard_map/ppermute | solution.py:121
  409.3 3.6 copy-start.13
  409.3 3.6 copy-start.35
  412.6 4.5 collective-permute-start.1
  417.2 40.3 %copy-start.48 = (bf16[48,2048]{1,0:T(8,128)(2,1)S(1)}, bf16[48,2048]{1,0:T(8,128)(2,1)}, u32[]{:S(2)}) copy-start(bf16[48,2048]{1,0:T(8,128)(2,1)} %reduce-scatter.11.cloned.1.call-done) | copy-start | bytes 589828
  417.2 16.4 %collective-permute-start.4 = (bf16[48,2048]{1,0:T(8,128)(2,1)}, bf16[48,2048]{1,0:T(8,128)(2,1)S(1)}, u32[]{:S(2)}, u32[]{:S(2)}) collective-permute-start(bf16[48,2048]{1,0:T(8,128)(2,1)} %reduce-scatter.11.cloned.1.call-done), channel_id=1, source_target_pairs={{0,24},{8,0},{16,8},{24,16},{1,25},{9,1},{17,9},{25,17},{2,26},{10... | collective-permute-start | bytes 589832 | tf_op jit(solution)/shard_map/ppermute | solution.py:121
  434.6 22.1 %collective-permute-start.5 = (bf16[96,2048]{1,0:T(8,128)(2,1)S(1)}, bf16[96,2048]{1,0:T(8,128)(2,1)S(1)}, u32[]{:S(2)}, u32[]{:S(2)}) collective-permute-start(bf16[96,2048]{1,0:T(8,128)(2,1)S(1)} %pad_maximum_fusion.3), channel_id=1, source_target_pairs={{0,16},{8,24},{16,0},{24,8},{1,17},{9,25},{17,1},{25,9},{2,18},{10... | collective-permute-start | bytes 1179656 | tf_op jit(solution)/shard_map/ppermute | solution.py:121
  444.6 20.7 %collective-permute-start.2 = (bf16[256,768]{1,0:T(8,128)(2,1)}, bf16[256,768]{1,0:T(8,128)(2,1)S(1)}, u32[]{:S(2)}, u32[]{:S(2)}) collective-permute-start(bf16[256,768]{1,0:T(8,128)(2,1)} %reduce-scatter.7.cloned.1.call-done), channel_id=1, source_target_pairs={{0,24},{8,0},{16,8},{24,16},{1,25},{9,1},{17,9},{25,17},{2,26},{10... | collective-permute-start | bytes 1179656 | tf_op jit(solution)/shard_map/ppermute | solution.py:121
  466.4 39.7 %collective-permute-start.3 = (bf16[512,768]{1,0:T(8,128)(2,1)S(1)}, bf16[512,768]{1,0:T(8,128)(2,1)S(1)}, u32[]{:S(2)}, u32[]{:S(2)}) collective-permute-start(bf16[512,768]{1,0:T(8,128)(2,1)S(1)} %pad_maximum_fusion.2), channel_id=1, source_target_pairs={{0,16},{8,24},{16,0},{24,8},{1,17},{9,25},{17,1},{25,9},{2,18},{10... | collective-permute-start | bytes 2359304 | tf_op jit(solution)/shard_map/ppermute | solution.py:121
  473.7 3.3 copy-start.36
  (45 other events, 73.4 us)
Sparse Core Ops, SparseCore 0:
  10.6 48.4 all-gather.7
  61.0 72.1 all-gather.5
  216.0 61.7 reduce-scatter.8
  281.5 92.3 reduce-scatter.4
  376.2 23.3 reduce-scatter.10
  401.9 42.6 reduce-scatter.6
